TPU v7x, 128 devices: a whole 4x4x4 slice. The times are simulated.
128 devices in a mesh: dp: 128 (over y, x, z, core).
Axes of the slice: x: 4, y: 4, z: 4, core: 2. Of those that a mesh axis runs over, the one named last changes fastest.
Arguments:
- features: bfloat16 [128, 128, 8, 2048], P('dp'), may hold values from -12 to 14, as said below
- slot_mask: int32 [128, 128, 8], P('dp'), may hold values from 0 to 1, as said below
- owner: int32 [128], replicated, may hold values from 0 to 127, each once
Outputs:
- class_mean: float32 [128, 2048], P('dp')
- class_cov: float32 [128, 2048, 2048], P('dp')
Inputs may be any that keep to these rules, and one draw needn't show every extreme that they name: `slot_mask`: every class has one device whose block of that class is full, so each class counts at least 8 images; about two thirds of slots hold images, with a fill rate that differs from class to class. The features of a class scatter around a class mean.
All inputs are finite; a program needn't handle non-finite values.
Results may differ from a plain program's by a relative error of at most 0.0003.
Values may be sent and summed in bfloat16 or wider, within the bound.
A program may use at most 64 MiB of HBM per device.

v0:
```python
import jax
import jax.numpy as jnp
from jax import lax
from jax.sharding import PartitionSpec as P


def local(features, slot_mask, owner):
    devices = lax.axis_size("dp")
    blocks = features[0]
    weights = slot_mask[0]
    index = jnp.arange(devices, dtype=jnp.int32)
    match = (owner[None, :] == index[:, None]).astype(jnp.int32)
    class_of = jnp.sum(match * index[None, :], axis=1)
    ordered = jnp.take(blocks, class_of, axis=0)
    ordered_weights = jnp.take(weights, class_of, axis=0)
    arrived, arrived_weights = (
        lax.all_to_all(ordered, "dp", split_axis=0, concat_axis=0, tiled=True),
        lax.all_to_all(ordered_weights, "dp", split_axis=0, concat_axis=0, tiled=True),
    )
    width = arrived.shape[-1]
    rows = arrived.reshape(-1, width)
    slot_weight = arrived_weights.reshape(-1).astype(jnp.float32)
    count = jnp.sum(slot_weight)
    weight_row = slot_weight.astype(jnp.bfloat16)[None, :]
    mean = jnp.dot(weight_row, rows, preferred_element_type=jnp.float32)[0] / count
    weighted = rows * weight_row[0][:, None]
    second = lax.dot_general(
        weighted, rows, (((0,), (0,)), ((), ())), preferred_element_type=jnp.float32
    )
    cov = (second - count * mean[:, None] * mean[None, :]) / (count - 1.0)
    return (mean[None, :], cov[None, :, :])


def solution(mesh):
    return jax.shard_map(
        local,
        mesh=mesh,
        in_specs=(P("dp", None, None, None), P("dp", None, None), P()),
        out_specs=(P("dp", None), P("dp", None, None)),
        check_vma=False,
    )
```

profile of v0, /device:TPU:0, one launch (start us, length us, event | category | flops | bytes accessed | tf_op | source)
XLA Modules:
  0.0 107.0 jit_solution(14439763944164429092)
XLA Ops:
  0.6 0.8 select_reduce_fusion
  1.4 0.8 copy.20
  2.2 0.6 gather_fusion
  2.9 0.7 bitcast_select_fusion
  3.6 11.2 %all-to-all-start = ((s32[128,1,8]{2,1,0:T(1,128)}), s32[128,1,8]{2,1,0:T(1,128)S(1)}, u32[]{:S(2)}, u32[]{:S(2)}) async-start(s32[128,1,8]{2,1,0:T(1,128)} %bitcast.4), calls=%async_computation | async-start | bytes 131072 | tf_op jit(solution)/shard_map/all_to_all | solution.py:18
  14.7 5.0 %gather_fusion.1 = bf16[128,8,2048]{2,1,0:T(8,128)(2,1)} fusion(bf16[128,8,2048]{2,1,0:T(8,128)(2,1)} %bitcast.27, s32[1024]{0:T(1024)S(1)} %pad_clamp_fusion), kind=kCustom, calls=%fused_computation.1 | custom fusion | bytes 8389120 | tf_op jit(solution)/shard_map/jit(_take)/gather | solution.py:14
  19.8 4.6 %broadcast_select_fusion = bf16[128,8,2048]{2,1,0:T(8,128)(2,1)} fusion(bf16[128,8,2048]{2,1,0:T(8,128)(2,1)} %gather_fusion.1, pred[128]{0:T(512)(128)(4,1)S(1)} %compare_and_fusion), kind=kLoop, calls=%fused_computation.6 | loop fusion | flops 2097152 | bytes 8388736 | tf_op jit(solution)/shard_map/jit(_take)/select_n | solution.py:14
  24.4 0.0 all-to-all-done
  24.4 10.3 %all-to-all-start.1 = ((bf16[128,8,2048]{2,1,0:T(8,128)(2,1)}), bf16[128,8,2048]{2,1,0:T(8,128)(2,1)}, u32[]{:S(2)}, u32[]{:S(2)}) async-start(bf16[128,8,2048]{2,1,0:T(8,128)(2,1)} %broadcast_select_fusion), calls=%async_computation.1 | async-start | bytes 8388608 | tf_op jit(solution)/shard_map/all_to_all | solution.py:17
  34.8 0.1 copy.23
  34.9 0.1 copy.24
  35.0 0.6 convert_reduce_fusion
  36.3 50.9 %all-to-all-done.1 = bf16[128,8,2048]{2,1,0:T(8,128)(2,1)} async-done(((bf16[128,8,2048]{2,1,0:T(8,128)(2,1)}), bf16[128,8,2048]{2,1,0:T(8,128)(2,1)}, u32[]{:S(2)}, u32[]{:S(2)}) %all-to-all-start.1) | async-done | bytes 4194336 | tf_op jit(solution)/shard_map/all_to_all | solution.py:17
  87.2 3.1 %fusion.7 = f32[1,2048,1]{1,0,2:T(1,128)S(1)} fusion(bf16[128,8,1]{1,2,0:T(2,128)(2,1)S(1)} %copy.24, bf16[128,8,2048]{2,1,0:T(8,128)(2,1)} %all-to-all-done.1), kind=kOutput, calls=%fused_computation.22 | convolution fusion | flops 4194304 | bytes 4204544 | tf_op jit(solution)/shard_map/dot_general | solution.py:25
  90.3 0.7 broadcast_multiply_fusion
  90.9 0.0 copy-start
  91.0 16.1 %fusion.1 = f32[1,2048,2048]{2,1,0:T(8,128)} fusion(bf16[128,8,2048]{2,1,0:T(8,128)(2,1)} %all-to-all-done.1, f32[]{:T(128)S(6)} %sub.7, f32[2048]{0:T(1024)S(1)} %get-tuple-element.3, f32[2048]{0:T(1024)S(1)} %get-tuple-element.2, bf16[128,8]{1,0:T(8,128)(2,1)S(1)} %copy.23), kind=kOutput, calls=%fused_computation.4 | convolution fusion | flops 8604614656 | bytes 20989956 | tf_op jit(solution)/shard_map/dot_general | solution.py:27
  107.0 0.0 copy-done
  (5 shorter events, 0.1 us)
Async XLA Ops:
  3.6 20.8 %all-to-all-start = ((s32[128,1,8]{2,1,0:T(1,128)}), s32[128,1,8]{2,1,0:T(1,128)S(1)}, u32[]{:S(2)}, u32[]{:S(2)}) async-start(s32[128,1,8]{2,1,0:T(1,128)} %bitcast.4), calls=%async_computation | async-start | bytes 131072 | tf_op jit(solution)/shard_map/all_to_all | solution.py:18
  24.4 62.8 %all-to-all-start.1 = ((bf16[128,8,2048]{2,1,0:T(8,128)(2,1)}), bf16[128,8,2048]{2,1,0:T(8,128)(2,1)}, u32[]{:S(2)}, u32[]{:S(2)}) async-start(bf16[128,8,2048]{2,1,0:T(8,128)(2,1)} %broadcast_select_fusion), calls=%async_computation.1 | async-start | bytes 8388608 | tf_op jit(solution)/shard_map/all_to_all | solution.py:17
  90.9 16.1 %copy-start = (f32[2048]{0:T(1024)}, f32[2048]{0:T(1024)S(1)}, u32[]{:S(2)}) copy-start(f32[2048]{0:T(1024)S(1)} %get-tuple-element.3) | copy-start | bytes 24580
where the time goes:
time: 107 us
  waiting for transfers between devices  50.9 us (48%)
  starting transfers between devices  21.5 us (20%)
  matrix products  19.1 us (18%)
  other arithmetic  7.39 us (7%)
  local copies, waits for them, and re-layouts  6.77 us (6%)
  between operations  1.36 us (1%)
    all_to_all x1, waiting for transfers between devices, local(): lax.all_to_all(ordered, 'dp', split_axis=0, concat_axis=0, tiled=True)  50.9 us
    dot_general x1, matrix products, local(): lax.dot_general(weighted, rows, (((0,), (0,)), ((), ())), preferred_eleme...  16.1 us
    all_to_all x1, starting transfers between devices, local(): lax.all_to_all(ordered_weights, 'dp', split_axis=0, concat_axis=0, tiled=...  11.2 us
    all_to_all x1, starting transfers between devices, local(): lax.all_to_all(ordered, 'dp', split_axis=0, concat_axis=0, tiled=True)  10.3 us
    gather x1, local copies, waits for them, and re-layouts, local(): ordered = jnp.take(blocks, class_of, axis=0)  5.02 us
    select_n x1, other arithmetic, local(): ordered = jnp.take(blocks, class_of, axis=0)  4.65 us
    dot_general x1, matrix products, local(): jnp.dot(weight_row, rows, preferred_element_type=jnp.float32)[0] / count  3.05 us
  transfers between devices with their start and end apart: 2, of which 1 were waited for; matrix products, arithmetic and copies ran while one was open for 10% of the time, Pallas kernels for 0%

commit v1 on v0

v1 whole, which is shorter than its diff:
```python
import jax
import jax.numpy as jnp
from jax import lax
from jax.experimental import pallas as pl
from jax.experimental.pallas import tpu as pltpu
from jax.sharding import PartitionSpec as P

MESH = pl.DeviceIdType.MESH
N = 128
CAP = 8
F = 2048
GROUPS = (32, 32, 32, 16, 16)
LAST = GROUPS[-1]
STRIP = 256


def parts_of(index):
    return index // 32, (index // 8) % 4, (index // 2) % 4, index % 2


def shifted(me, shift):
    (y, x, z, c), (dy, dx, dz, dc) = parts_of(me), parts_of(shift)
    return ((y + dy) % 4) * 32 + ((x + dx) % 4) * 8 + ((z + dz) % 4) * 2 + (c + dc) % 2


def link_load(shift):
    load = [0] * 6
    for k, d in enumerate(parts_of(shift)[:3]):
        if d in (1, 2):
            load[2 * k] += 1
        if d in (3, 2):
            load[2 * k + 1] += 1
    return load


def send_order():
    rest, total, order = list(range(1, N)), [0] * 6, []

    def score(shift):
        after = [a + b for a, b in zip(total, link_load(shift))]
        mean = sum(after) / 6
        return sum((a - mean) ** 2 for a in after) - 3 * sum(link_load(shift)), (shift * 37) % N

    while rest:
        best = min(rest, key=score)
        rest.remove(best)
        order.append(best)
        total = [a + b for a, b in zip(total, link_load(best))]
    return order


ORDER = [0] + send_order()
STARTS = [sum(GROUPS[:g]) for g in range(len(GROUPS))]


def gather_kernel(class_of, mask_ref, feat_hbm, acc_ref, last_ref, sums_ref, count_ref,
                  feat, send, rows, xt, tally, tallies, feat_sem, send_sem, recv_sem, tally_send, tally_recv):
    me = lax.axis_index("dp")
    load = pltpu.make_async_copy(feat_hbm, feat, feat_sem)
    load.start()
    barrier = pltpu.get_barrier_semaphore()

    def greet(k, _):
        pl.semaphore_signal(barrier, inc=1, device_id=(lax.rem(me + k, N),), device_id_type=MESH)
        return 0

    lax.fori_loop(1, N, greet, 0)

    mask = mask_ref[...].astype(jnp.float32)
    tally[...] = jnp.sum(mask, axis=0, keepdims=True)
    lanes = lax.broadcasted_iota(jnp.int32, (CAP, N), 1)
    load.wait()

    def arrange(j, _):
        cls = class_of[j]
        weight = jnp.sum(jnp.where(lanes == cls, mask, 0.0), axis=1, keepdims=True)
        block = feat[cls].astype(jnp.float32) * weight
        send[j] = block.astype(jnp.bfloat16)
        return 0

    lax.fori_loop(0, N, arrange, 0, unroll=4)

    pl.semaphore_wait(barrier, N - 1)
    tally_copies = []
    for g, start in enumerate(STARTS):
        for k in range(max(start, 1), start + GROUPS[g]):
            to = shifted(me, ORDER[k])
            pltpu.make_async_remote_copy(
                send.at[to], rows.at[k], send_sem, recv_sem.at[g], device_id=(to,), device_id_type=MESH
            ).start()
            copy = pltpu.make_async_remote_copy(
                tally, tallies.at[pl.ds(k, 1)], tally_send, tally_recv, device_id=(to,), device_id_type=MESH
            )
            copy.start()
    rows[0] = send[me]
    tallies[pl.ds(0, 1)] = tally[...]

    for g, start in enumerate(STARTS):
        first = max(start, 1)
        size = start + GROUPS[g] - first
        pltpu.make_async_remote_copy(
            send.at[pl.ds(first, size)], rows.at[pl.ds(first, size)], send_sem, recv_sem.at[g],
            device_id=(me,), device_id_type=MESH,
        ).wait_recv()
        depth = GROUPS[g] * CAP
        x = rows[pl.ds(start, GROUPS[g])].reshape(depth, F)
        total = jnp.sum(x.astype(jnp.float32), axis=0, keepdims=True)
        if g == 0:
            sums_ref[...] = total
        else:
            sums_ref[...] += total
        if g == len(GROUPS) - 1:
            last_ref[...] = x
            continue
        xt[:, pl.ds(0, depth)] = x.T

        def strip(i, _, depth=depth, g=g, start=start):
            at = pl.ds(pl.multiple_of(i * STRIP, STRIP), STRIP)
            right = rows[pl.ds(start, GROUPS[g]), :, at].reshape(depth, STRIP)
            product = jnp.dot(xt[:, pl.ds(0, depth)], right, preferred_element_type=jnp.float32)
            if g == 0:
                acc_ref[:, at] = product
            else:
                acc_ref[:, at] += product
            return 0

        lax.fori_loop(0, F // STRIP, strip, 0)

    pltpu.make_async_remote_copy(
        send.at[pl.ds(1, N - 1)], rows.at[pl.ds(1, N - 1)], send_sem, recv_sem.at[0],
        device_id=(me,), device_id_type=MESH,
    ).wait_send()
    done = pltpu.make_async_remote_copy(
        tallies.at[pl.ds(1, N - 1)], tallies.at[pl.ds(1, N - 1)], tally_send, tally_recv,
        device_id=(me,), device_id_type=MESH,
    )
    done.wait_send()
    done.wait_recv()
    mine = jnp.where(lax.broadcasted_iota(jnp.int32, (N, N), 1) == class_of[me], tallies[...], 0.0)
    count_ref[0, 0] = jnp.sum(mine)


def finish_kernel(count_ref, acc_ref, last_ref, sums_ref, mean_ref, cov_hbm, lt, stage, sems):
    count = count_ref[0, 0]
    mean = sums_ref[...] / count
    mean_ref[...] = mean
    scale = 1.0 / (count - 1.0)
    lt[...] = last_ref[...].T
    column = (mean * jnp.ones((8, 1), jnp.float32)).T[:, :1]

    def out(i):
        return pltpu.make_async_copy(stage.at[i % 2], cov_hbm.at[0, pl.ds(i * STRIP, STRIP)], sems.at[i % 2])

    for i in range(F // STRIP):
        at = pl.ds(i * STRIP, STRIP)
        if i >= 2:
            out(i - 2).wait()
        product = jnp.dot(lt[at, :], last_ref[...], preferred_element_type=jnp.float32)
        left = lax.slice(column, (i * STRIP, 0), ((i + 1) * STRIP, 1)) * count
        stage[i % 2] = (acc_ref[at, :] + product - left * mean) * scale
        out(i).start()
    out(F // STRIP - 2).wait()
    out(F // STRIP - 1).wait()


def local(features, slot_mask, owner):
    index = jnp.arange(N, dtype=jnp.int32)
    match = (owner[None, :] == index[:, None]).astype(jnp.int32)
    class_of = jnp.sum(match * index[None, :], axis=1)
    vmem = pl.BlockSpec(memory_space=pltpu.VMEM)
    smem = pl.BlockSpec(memory_space=pltpu.SMEM)
    hbm = pl.BlockSpec(memory_space=pl.ANY)
    acc, last, sums, count = pl.pallas_call(
        gather_kernel,
        out_shape=(
            pltpu.VMEM((F, F), jnp.float32),
            pltpu.VMEM((LAST * CAP, F), jnp.bfloat16),
            pltpu.VMEM((1, F), jnp.float32),
            jax.ShapeDtypeStruct((1, 1), jnp.float32),
        ),
        in_specs=[smem, vmem, hbm],
        out_specs=(vmem, vmem, vmem, smem),
        scratch_shapes=[
            pltpu.VMEM((N, CAP, F), jnp.bfloat16),
            pltpu.VMEM((N, CAP, F), jnp.bfloat16),
            pltpu.VMEM((N, CAP, F), jnp.bfloat16),
            pltpu.VMEM((F, max(GROUPS) * CAP), jnp.bfloat16),
            pltpu.VMEM((1, N), jnp.float32),
            pltpu.VMEM((N, N), jnp.float32),
            pltpu.SemaphoreType.DMA,
            pltpu.SemaphoreType.DMA,
            pltpu.SemaphoreType.DMA((len(GROUPS),)),
            pltpu.SemaphoreType.DMA,
            pltpu.SemaphoreType.DMA,
        ],
        compiler_params=pltpu.CompilerParams(
            collective_id=0, has_side_effects=True, vmem_limit_bytes=40 * 1024 * 1024
        ),
        name="gather",
    )(class_of, slot_mask[0].T, features[0])
    mean, cov = pl.pallas_call(
        finish_kernel,
        out_shape=(jax.ShapeDtypeStruct((1, F), jnp.float32), jax.ShapeDtypeStruct((1, F, F), jnp.float32)),
        in_specs=[smem, vmem, vmem, vmem],
        out_specs=(vmem, hbm),
        scratch_shapes=[
            pltpu.VMEM((F, LAST * CAP), jnp.bfloat16),
            pltpu.VMEM((2, STRIP, F), jnp.float32),
            pltpu.SemaphoreType.DMA((2,)),
        ],
        compiler_params=pltpu.CompilerParams(vmem_limit_bytes=20 * 1024 * 1024),
        name="finish",
    )(count, *(pltpu.with_memory_space_constraint(a, pltpu.VMEM) for a in (acc, last, sums)))
    return mean, cov


def solution(mesh):
    return jax.shard_map(
        local,
        mesh=mesh,
        in_specs=(P("dp", None, None, None), P("dp", None, None), P()),
        out_specs=(P("dp", None), P("dp", None, None)),
        check_vma=False,
    )
```

time: 107 us -> 78.5 us (0.73)
  Pallas kernels: 0 us -> 76.4 us
  waiting for transfers between devices: 50.9 us -> 0 us
  starting transfers between devices: 21.5 us -> 0 us
  matrix products: 19.1 us -> 0 us
  local copies, waits for them, and re-layouts: 6.77 us -> 0 us
  other arithmetic: 7.39 us -> 1.28 us
    pallas_call x0 -> x2, Pallas kernels: none -> 76.4 us  [the longest x1 66.8 us: local(): pl.pallas_call(gather_kernel, out_shape=(pltpu.VMEM((F, F), jnp.float32),...]
    all_to_all x2 -> x0, waiting for transfers between devices: 50.9 us -> none  [the longest x1 50.9 us: local(): lax.all_to_all(ordered, 'dp', split_axis=0, concat_axis=0, tiled=True)]
    all_to_all x2 -> x0, starting transfers between devices: 21.5 us -> none  [the longest x1 11.2 us: local(): lax.all_to_all(ordered_weights, 'dp', split_axis=0, concat_axis=0, tiled=...]
    dot_general x2 -> x0, matrix products: 19.1 us -> none  [the longest x1 16.1 us: local(): lax.dot_general(weighted, rows, (((0,), (0,)), ((), ())), preferred_eleme...]
    gather x2 -> x0, local copies, waits for them, and re-layouts: 5.66 us -> none  [the longest x1 5.02 us: local(): ordered = jnp.take(blocks, class_of, axis=0)]
    select_n x3 -> x0, other arithmetic: 5.35 us -> none  [the longest x1 4.65 us: local(): ordered = jnp.take(blocks, class_of, axis=0)]
  transfers between devices with their start and end apart: 2 -> 0, of which waited for: 1 -> 0; matrix products, arithmetic and copies ran while one was open for 10% -> 0% of each run, Pallas kernels for 0% -> 0%
where the time goes in v1:
time: 78.5 us; the launch traced here: 78.3 us
  Pallas kernels  76.4 us (97%)
  other arithmetic  1.28 us (2%)
    pallas_call x1, Pallas kernels, local(): pl.pallas_call(gather_kernel, out_shape=(pltpu.VMEM((F, F), jnp.float32),...  66.8 us
    pallas_call x1, Pallas kernels, local(): pl.pallas_call(finish_kernel, out_shape=(jax.ShapeDtypeStruct((1, F), jnp...  9.6 us

profile of v1, /device:TPU:0, one launch (start us, length us, event | category | flops | bytes accessed | tf_op | source)
XLA Modules:
  0.0 78.3 jit_solution(4496745768150860533)
XLA Ops:
  0.6 1.3 %select_reduce_fusion.class_of = s32[128]{0:T(128)} fusion(s32[128]{0:T(128)} %param.5), kind=kLoop, calls=%fused_computation | loop fusion | flops 49024 | bytes 1024 | tf_op jit(solution)/shard_map/reduce_sum | solution.py:169
  1.9 66.8 %gather.1 = (f32[2048,2048]{1,0:T(8,128)S(1)}, bf16[128,2048]{1,0:T(8,128)(2,1)S(1)}, f32[1,2048]{1,0:T(1,128)S(1)}, f32[1,1]{1,0:T(1,128)}) custom-call(s32[128]{0:T(128)} %select_reduce_fusion.class_of, s32[8,128]{1,0:T(8,128)} %bitcast.5, bf16[128,8,2048]{2,1,0:T(8,128)(2,1)} %bitcast.4), custom_call_target="tpu_custom_call" | custom-call | tf_op jit(solution)/shard_map/gather/pallas_call | solution.py:173
  68.7 9.6 %finish.1 = (f32[1,2048]{1,0:T(1,128)}, f32[1,2048,2048]{2,1,0:T(8,128)}) custom-call(f32[1,1]{1,0:T(1,128)} %get-tuple-element.6.count_ref, f32[2048,2048]{1,0:T(8,128)S(1)} %get-tuple-element.7.acc_ref, bf16[128,2048]{1,0:T(8,128)(2,1)S(1)} %get-tuple-element.8.last_ref, f32[1,2048]{1,0:T(1,128)S(1)} %get-tuple-element.9.sums_ref), custom_call_target="tpu_custom_call" | custom-call | tf_op jit(solution)/shard_map/finish/pallas_call | solution.py:201

commit v2 on v1

v2 whole, which is shorter than its diff:
```python
import jax
import jax.numpy as jnp
from jax import lax
from jax.experimental import pallas as pl
from jax.experimental.pallas import tpu as pltpu
from jax.sharding import PartitionSpec as P

MESH = pl.DeviceIdType.MESH
N = 128
CAP = 8
F = 2048
GROUPS = (32, 32, 32, 16, 8, 8)
ADDED = 3
LAST = sum(GROUPS[ADDED:]) * CAP
STRIP = 256
OUT_STRIPS = (128, 128) + (256,) * 7


def parts_of(index):
    return index // 32, (index // 8) % 4, (index // 2) % 4, index % 2


def shifted(me, shift):
    (y, x, z, c), (dy, dx, dz, dc) = parts_of(me), parts_of(shift)
    return ((y + dy) % 4) * 32 + ((x + dx) % 4) * 8 + ((z + dz) % 4) * 2 + (c + dc) % 2


def partner(me, shift):
    (y, x, z, c), (*ways, dc) = parts_of(me), parts_of(shift)
    dy, dx, dz = (ways[k] + ((4 - ways[(k + 1) % 3]) % 4 - ways[k]) * c for k in range(3))
    return ((y + dy) % 4) * 32 + ((x + dx) % 4) * 8 + ((z + dz) % 4) * 2 + (c + dc) % 2


def link_load(shift):
    load = [0] * 6
    for k, d in enumerate(parts_of(shift)[:3]):
        if d in (1, 2):
            load[2 * k] += 1
        if d in (3, 2):
            load[2 * k + 1] += 1
    return load


def hops(shift):
    return sum(link_load(shift))


def send_order(round_of):
    rest, total, order = list(range(1, N)), [0] * 6, []

    def score(shift):
        after = [a + b for a, b in zip(total, link_load(shift))]
        mean = sum(after) / 6
        return round_of(shift), sum((a - mean) ** 2 for a in after), (shift * 37) % N

    while rest:
        best = min(rest, key=score)
        rest.remove(best)
        order.append(best)
        total = [a + b for a, b in zip(total, link_load(best))]
    return order


RADIUS = 1
ROUNDS = 6


def round_of(shift):
    return max(hops(shift), 1) if hops(shift) <= 2 else ROUNDS


ORDER = [0] + send_order(round_of)
STARTS = [sum(GROUPS[:g]) for g in range(len(GROUPS))]
NEAR = sorted((shift for shift in range(1, N) if hops(shift) <= RADIUS), key=lambda shift: -hops(shift))


def gather_kernel(owner_hbm, mask_hbm, feat_hbm, acc_ref, last_ref, turned_ref, sums_ref, count_ref,
                  owner, mask_in, class_row, class_of, feat, send, rows, xt, tally, tallies,
                  in_sems, send_sem, recv_sem, tally_send, tally_recv, round_sems):
    me = lax.axis_index("dp")
    fetches = [
        pltpu.make_async_copy(src, dst, in_sems.at[i])
        for i, (src, dst) in enumerate(((owner_hbm, owner), (mask_hbm, mask_in), (feat_hbm, feat)))
    ]
    for fetch in fetches:
        fetch.start()
    barrier = pltpu.get_barrier_semaphore()
    for shift in NEAR:
        pl.semaphore_signal(barrier, inc=1, device_id=(shifted(me, shift),), device_id_type=MESH)

    fetches[0].wait()
    square = (N, N)
    owner_of_row = jnp.broadcast_to(owner[...], square).T
    matches = owner_of_row == lax.broadcasted_iota(jnp.int32, square, 1)
    class_row[...] = jnp.max(
        jnp.where(matches, lax.broadcasted_iota(jnp.int32, square, 0), 0), axis=0, keepdims=True
    )
    to_scalars = pltpu.make_async_copy(class_row, class_of, in_sems.at[3])
    to_scalars.start()
    fetches[1].wait()
    mask = mask_in[...].astype(jnp.float32)
    tally[...] = jnp.sum(mask, axis=0, keepdims=True)
    lanes = lax.broadcasted_iota(jnp.int32, (CAP, N), 1)
    to_scalars.wait()

    def finish_round(r):
        pl.semaphore_wait(barrier if r == 1 else round_sems.at[r - 2], len(NEAR))
        if r < ROUNDS:
            for shift in NEAR:
                pl.semaphore_signal(
                    round_sems.at[r - 1], inc=1, device_id=(shifted(me, shift),), device_id_type=MESH
                )

    finish_round(1)
    fetches[2].wait()

    def masked(j):
        cls = class_of[0, j]
        weight = jnp.sum(jnp.where(lanes == cls, mask, 0.0), axis=1, keepdims=True)
        return (feat[cls].astype(jnp.float32) * weight).astype(jnp.bfloat16)

    for r in range(1, ROUNDS + 1):
        slots = [k for k in range(1, N) if round_of(ORDER[k]) == r]
        for k in slots:
            to = partner(me, ORDER[k])
            send[to] = masked(to)
        if r > 1:
            finish_round(r)
        for k in slots:
            to = partner(me, ORDER[k])
            g = max(g for g, start in enumerate(STARTS) if start <= k)
            pltpu.make_async_remote_copy(
                send.at[to], rows.at[k], send_sem, recv_sem.at[g], device_id=(to,), device_id_type=MESH
            ).start()
            pltpu.make_async_remote_copy(
                tally, tallies.at[pl.ds(k, 1)], tally_send, tally_recv, device_id=(to,), device_id_type=MESH
            ).start()
    rows[0] = masked(me)
    tallies[pl.ds(0, 1)] = tally[...]

    for g, start in enumerate(STARTS):
        first = max(start, 1)
        size = start + GROUPS[g] - first
        pltpu.make_async_remote_copy(
            send.at[pl.ds(first, size)], rows.at[pl.ds(first, size)], send_sem, recv_sem.at[g],
            device_id=(me,), device_id_type=MESH,
        ).wait_recv()
        depth = GROUPS[g] * CAP
        x = rows[pl.ds(start, GROUPS[g])].reshape(depth, F)
        total = jnp.sum(x.astype(jnp.float32), axis=0, keepdims=True)
        if g == 0:
            sums_ref[...] = total
        else:
            sums_ref[...] += total
        if g >= ADDED:
            at = pl.ds((start - STARTS[ADDED]) * CAP, depth)
            last_ref[at] = x
            turned_ref[:, at] = x.T
            continue
        xt[:, pl.ds(0, depth)] = x.T

        def strip(i, _, depth=depth, g=g, start=start):
            at = pl.ds(pl.multiple_of(i * STRIP, STRIP), STRIP)
            right = rows[pl.ds(start, GROUPS[g]), :, at].reshape(depth, STRIP)
            product = jnp.dot(xt[:, pl.ds(0, depth)], right, preferred_element_type=jnp.float32)
            if g == 0:
                acc_ref[:, at] = product
            else:
                acc_ref[:, at] += product
            return 0

        lax.fori_loop(0, F // STRIP, strip, 0)

    pltpu.make_async_remote_copy(
        send.at[pl.ds(1, N - 1)], rows.at[pl.ds(1, N - 1)], send_sem, recv_sem.at[0],
        device_id=(me,), device_id_type=MESH,
    ).wait_send()
    done = pltpu.make_async_remote_copy(
        tallies.at[pl.ds(1, N - 1)], tallies.at[pl.ds(1, N - 1)], tally_send, tally_recv,
        device_id=(me,), device_id_type=MESH,
    )
    done.wait_send()
    done.wait_recv()
    mine = jnp.where(lax.broadcasted_iota(jnp.int32, square, 1) == class_of[0, me], tallies[...], 0.0)
    count_ref[...] = jnp.broadcast_to(jnp.sum(jnp.sum(mine, axis=0, keepdims=True), axis=1, keepdims=True), (1, N))


def finish_kernel(acc_ref, last_ref, turned_ref, sums_ref, count_ref, mean_hbm, cov_hbm, mean_ref, stage, sems):
    count = count_ref[:, :1]
    sums = sums_ref[...]
    mean = sums / count
    mean_ref[...] = mean
    copies = [pltpu.make_async_copy(mean_ref, mean_hbm, sems.at[len(OUT_STRIPS)])]
    copies[0].start()
    scale = 1.0 / (count - 1.0)
    start = 0
    for i, size in enumerate(OUT_STRIPS):
        at = pl.ds(start, size)
        product = jnp.dot(turned_ref[at, :], last_ref[...], preferred_element_type=jnp.float32)
        left = jnp.broadcast_to(sums_ref[:, at], (8, size)).T[:, :1]
        stage[at, :] = (acc_ref[at, :] + product - left * mean) * scale
        copies.append(pltpu.make_async_copy(stage.at[at], cov_hbm.at[0, at], sems.at[i]))
        copies[-1].start()
        start += size
    for copy in copies:
        copy.wait()


def local(features, slot_mask, owner):
    vmem = pl.BlockSpec(memory_space=pltpu.VMEM)
    hbm = pl.BlockSpec(memory_space=pl.ANY)
    partial_sums = pl.pallas_call(
        gather_kernel,
        out_shape=(
            pltpu.VMEM((F, F), jnp.float32),
            pltpu.VMEM((LAST, F), jnp.bfloat16),
            pltpu.VMEM((F, LAST), jnp.bfloat16),
            pltpu.VMEM((1, F), jnp.float32),
            pltpu.VMEM((1, N), jnp.float32),
        ),
        in_specs=[pl.BlockSpec(memory_space=pltpu.HBM)] * 3,
        out_specs=(vmem,) * 5,
        scratch_shapes=[
            pltpu.VMEM((1, N), jnp.int32),
            pltpu.VMEM((CAP, N), jnp.int32),
            pltpu.VMEM((1, N), jnp.int32),
            pltpu.SMEM((1, N), jnp.int32),
            pltpu.VMEM((N, CAP, F), jnp.bfloat16),
            pltpu.VMEM((N, CAP, F), jnp.bfloat16),
            pltpu.VMEM((N, CAP, F), jnp.bfloat16),
            pltpu.VMEM((F, max(GROUPS) * CAP), jnp.bfloat16),
            pltpu.VMEM((1, N), jnp.float32),
            pltpu.VMEM((N, N), jnp.float32),
            pltpu.SemaphoreType.DMA((4,)),
            pltpu.SemaphoreType.DMA,
            pltpu.SemaphoreType.DMA((len(GROUPS),)),
            pltpu.SemaphoreType.DMA,
            pltpu.SemaphoreType.DMA,
            pltpu.SemaphoreType.REGULAR((ROUNDS - 1,)),
        ],
        compiler_params=pltpu.CompilerParams(
            collective_id=0, has_side_effects=True, vmem_limit_bytes=24 * 1024 * 1024
        ),
        name="gather",
    )(*(pltpu.with_memory_space_constraint(a, pltpu.HBM) for a in (owner[None, :], slot_mask[0].T, features[0])))
    mean, cov = pl.pallas_call(
        finish_kernel,
        out_shape=(jax.ShapeDtypeStruct((1, F), jnp.float32), jax.ShapeDtypeStruct((1, F, F), jnp.float32)),
        in_specs=[vmem] * 5,
        out_specs=(hbm, hbm),
        scratch_shapes=[
            pltpu.VMEM((1, F), jnp.float32),
            pltpu.VMEM((F, F), jnp.float32),
            pltpu.SemaphoreType.DMA((len(OUT_STRIPS) + 1,)),
        ],
        compiler_params=pltpu.CompilerParams(vmem_limit_bytes=28 * 1024 * 1024),
        name="finish",
    )(*(pltpu.with_memory_space_constraint(a, pltpu.VMEM) for a in partial_sums))
    return mean, cov


def solution(mesh):
    return jax.shard_map(
        local,
        mesh=mesh,
        in_specs=(P("dp", None, None, None), P("dp", None, None), P()),
        out_specs=(P("dp", None), P("dp", None, None)),
        check_vma=False,
    )
```

time: 78.5 us -> 66 us (0.84); the launches traced: 78.3 us -> 64.8 us
  Pallas kernels: 76.4 us -> 64.1 us
  other arithmetic: 1.28 us -> 0 us
    pallas_call x1, Pallas kernels: 66.8 us -> 57.3 us  [local(): pl.pallas_call(gather_kernel, out_shape=(pltpu.VMEM((F, F), jnp.float32),...]
    pallas_call x1, Pallas kernels: 9.6 us -> 6.85 us  [local(): pl.pallas_call(finish_kernel, out_shape=(jax.ShapeDtypeStruct((1, F), jnp...]
    reduce_sum x1 -> x0, other arithmetic: 1.28 us -> none  [local(): class_of = jnp.sum(match * index[None, :], axis=1)]
where the time goes in v2:
time: 66 us; the launch traced here: 64.8 us
  Pallas kernels  64.1 us (97%)
    pallas_call x1, Pallas kernels, local(): pl.pallas_call(gather_kernel, out_shape=(pltpu.VMEM((F, F), jnp.float32),...  57.3 us
    pallas_call x1, Pallas kernels, local(): pl.pallas_call(finish_kernel, out_shape=(jax.ShapeDtypeStruct((1, F), jnp...  6.85 us

profile of v2, /device:TPU:0, one launch (start us, length us, event | category | flops | bytes accessed | tf_op | source)
XLA Modules:
  0.0 64.8 jit_solution(12902321822770384554)
XLA Ops:
  0.6 57.3 %gather.1 = (f32[2048,2048]{1,0:T(8,128)S(1)}, bf16[256,2048]{1,0:T(8,128)(2,1)S(1)}, bf16[2048,256]{1,0:T(8,128)(2,1)S(1)}, f32[1,2048]{1,0:T(1,128)S(1)}, f32[1,128]{1,0:T(1,128)S(1)}) custom-call(s32[1,128]{1,0:T(1,128)} %bitcast.7, s32[8,128]{1,0:T(8,128)} %bitcast.6, bf16[128,8,2048]{2,1,0:T(8,128)(2,1)} %bitcast.5), custom_call_target="tpu_custom_call" | custom-call | tf_op jit(solution)/shard_map/gather/pallas_call | solution.py:212
  57.9 6.9 %finish.1 = (f32[1,2048]{1,0:T(1,128)}, f32[1,2048,2048]{2,1,0:T(8,128)}) custom-call(f32[2048,2048]{1,0:T(8,128)S(1)} %get-tuple-element.7.acc_ref, bf16[256,2048]{1,0:T(8,128)(2,1)S(1)} %get-tuple-element.8.last_ref, bf16[2048,256]{1,0:T(8,128)(2,1)S(1)} %get-tuple-element.9.turned_ref, f32[1,2048]{1,0:T(1,128)S(1)} %get-tuple-element.10.sums_ref, ...), custom_call_target="tpu_custom_call" | custom-call | tf_op jit(solution)/shard_map/finish/pallas_call | solution.py:246

commit v3 on v2

--- a/solution.py
+++ b/solution.py
@@ -27,7 +27,7 @@
 
 def partner(me, shift):
     (y, x, z, c), (*ways, dc) = parts_of(me), parts_of(shift)
-    dy, dx, dz = (ways[k] + ((4 - ways[(k + 1) % 3]) % 4 - ways[k]) * c for k in range(3))
+    dy, dx, dz = (way + ((4 - way) % 4 - way) * c for way in ways)
     return ((y + dy) % 4) * 32 + ((x + dx) % 4) * 8 + ((z + dz) % 4) * 2 + (c + dc) % 2
 
 
@@ -51,7 +51,7 @@
     def score(shift):
         after = [a + b for a, b in zip(total, link_load(shift))]
         mean = sum(after) / 6
-        return round_of(shift), sum((a - mean) ** 2 for a in after), (shift * 37) % N
+        return round_of(shift) + (0, 0, 0, 1, 0.5, 0, 0)[hops(shift)], sum((a - mean) ** 2 for a in after), (shift * 37) % N
 
     while rest:
         best = min(rest, key=score)
@@ -61,7 +61,6 @@
     return order
 
 
-RADIUS = 1
 ROUNDS = 6
 
 
@@ -71,11 +70,13 @@
 
 ORDER = [0] + send_order(round_of)
 STARTS = [sum(GROUPS[:g]) for g in range(len(GROUPS))]
-NEAR = sorted((shift for shift in range(1, N) if hops(shift) <= RADIUS), key=lambda shift: -hops(shift))
+NEAR = [shift for shift in range(1, N) if hops(shift) <= 1]
+OTHER_CORE = 1
+TALLIED = [shift for shift in ORDER if shift % 2 == 0]
 
 
 def gather_kernel(owner_hbm, mask_hbm, feat_hbm, acc_ref, last_ref, turned_ref, sums_ref, count_ref,
-                  owner, mask_in, class_row, class_of, feat, send, rows, xt, tally, tallies,
+                  owner, mask_in, class_row, class_of, feat, send, rows, xt, tally, other_tally, chip_tally, tallies,
                   in_sems, send_sem, recv_sem, tally_send, tally_recv, round_sems):
     me = lax.axis_index("dp")
     fetches = [
@@ -119,6 +120,12 @@
         weight = jnp.sum(jnp.where(lanes == cls, mask, 0.0), axis=1, keepdims=True)
         return (feat[cls].astype(jnp.float32) * weight).astype(jnp.bfloat16)
 
+    def send_tally(k):
+        pltpu.make_async_remote_copy(
+            chip_tally, tallies.at[pl.ds(TALLIED.index(ORDER[k]), 1)], tally_send.at[1], tally_recv.at[1],
+            device_id=(partner(me, ORDER[k]),), device_id_type=MESH,
+        ).start()
+
     for r in range(1, ROUNDS + 1):
         slots = [k for k in range(1, N) if round_of(ORDER[k]) == r]
         for k in slots:
@@ -126,17 +133,30 @@
             send[to] = masked(to)
         if r > 1:
             finish_round(r)
+        if r == 2:
+            other = pltpu.make_async_remote_copy(
+                tally, other_tally, tally_send.at[0], tally_recv.at[0], device_id=(me,), device_id_type=MESH
+            )
+            other.wait_send()
+            other.wait_recv()
+            chip_tally[...] = tally[...] + other_tally[...]
+            for k in range(1, slots[0]):
+                if ORDER[k] % 2 == 0:
+                    send_tally(k)
         for k in slots:
             to = partner(me, ORDER[k])
             g = max(g for g, start in enumerate(STARTS) if start <= k)
             pltpu.make_async_remote_copy(
                 send.at[to], rows.at[k], send_sem, recv_sem.at[g], device_id=(to,), device_id_type=MESH
             ).start()
-            pltpu.make_async_remote_copy(
-                tally, tallies.at[pl.ds(k, 1)], tally_send, tally_recv, device_id=(to,), device_id_type=MESH
-            ).start()
+            if ORDER[k] == OTHER_CORE:
+                pltpu.make_async_remote_copy(
+                    tally, other_tally, tally_send.at[0], tally_recv.at[0], device_id=(to,), device_id_type=MESH
+                ).start()
+            elif ORDER[k] % 2 == 0 and r > 1:
+                send_tally(k)
     rows[0] = masked(me)
-    tallies[pl.ds(0, 1)] = tally[...]
+    tallies[pl.ds(0, 1)] = chip_tally[...]
 
     for g, start in enumerate(STARTS):
         first = max(start, 1)
@@ -175,13 +195,14 @@
         send.at[pl.ds(1, N - 1)], rows.at[pl.ds(1, N - 1)], send_sem, recv_sem.at[0],
         device_id=(me,), device_id_type=MESH,
     ).wait_send()
+    others = tallies.at[pl.ds(1, len(TALLIED) - 1)]
     done = pltpu.make_async_remote_copy(
-        tallies.at[pl.ds(1, N - 1)], tallies.at[pl.ds(1, N - 1)], tally_send, tally_recv,
-        device_id=(me,), device_id_type=MESH,
+        others, others, tally_send.at[1], tally_recv.at[1], device_id=(me,), device_id_type=MESH
     )
     done.wait_send()
     done.wait_recv()
-    mine = jnp.where(lax.broadcasted_iota(jnp.int32, square, 1) == class_of[0, me], tallies[...], 0.0)
+    lanes = lax.broadcasted_iota(jnp.int32, (len(TALLIED), N), 1)
+    mine = jnp.where(lanes == class_of[0, me], tallies[...], 0.0)
     count_ref[...] = jnp.broadcast_to(jnp.sum(jnp.sum(mine, axis=0, keepdims=True), axis=1, keepdims=True), (1, N))
 
 
@@ -230,12 +251,14 @@
             pltpu.VMEM((N, CAP, F), jnp.bfloat16),
             pltpu.VMEM((F, max(GROUPS) * CAP), jnp.bfloat16),
             pltpu.VMEM((1, N), jnp.float32),
-            pltpu.VMEM((N, N), jnp.float32),
+            pltpu.VMEM((1, N), jnp.float32),
+            pltpu.VMEM((1, N), jnp.float32),
+            pltpu.VMEM((len(TALLIED), N), jnp.float32),
             pltpu.SemaphoreType.DMA((4,)),
             pltpu.SemaphoreType.DMA,
             pltpu.SemaphoreType.DMA((len(GROUPS),)),
-            pltpu.SemaphoreType.DMA,
-            pltpu.SemaphoreType.DMA,
+            pltpu.SemaphoreType.DMA((2,)),
+            pltpu.SemaphoreType.DMA((2,)),
             pltpu.SemaphoreType.REGULAR((ROUNDS - 1,)),
         ],
         compiler_params=pltpu.CompilerParams(

time: 66 us -> 65.7 us (level)
  no operation moved by 1% of the time
where the time goes in v3:
time: 65.7 us; the launch traced here: 64.8 us
  Pallas kernels  64.2 us (98%)
    pallas_call x1, Pallas kernels, local(): pl.pallas_call(gather_kernel, out_shape=(pltpu.VMEM((F, F), jnp.float32),...  57.3 us
    pallas_call x1, Pallas kernels, local(): pl.pallas_call(finish_kernel, out_shape=(jax.ShapeDtypeStruct((1, F), jnp...  6.85 us

profile of v3, /device:TPU:0, one launch (start us, length us, event | category | flops | bytes accessed | tf_op | source)
XLA Modules:
  0.0 64.8 jit_solution(10887271822087335821)
XLA Ops:
  0.6 57.3 %gather.1 = (f32[2048,2048]{1,0:T(8,128)S(1)}, bf16[256,2048]{1,0:T(8,128)(2,1)S(1)}, bf16[2048,256]{1,0:T(8,128)(2,1)S(1)}, f32[1,2048]{1,0:T(1,128)S(1)}, f32[1,128]{1,0:T(1,128)S(1)}) custom-call(s32[1,128]{1,0:T(1,128)} %bitcast.7, s32[8,128]{1,0:T(8,128)} %bitcast.6, bf16[128,8,2048]{2,1,0:T(8,128)(2,1)} %bitcast.5), custom_call_target="tpu_custom_call" | custom-call | tf_op jit(solution)/shard_map/gather/pallas_call | solution.py:233
  58.0 6.9 %finish.1 = (f32[1,2048]{1,0:T(1,128)}, f32[1,2048,2048]{2,1,0:T(8,128)}) custom-call(f32[2048,2048]{1,0:T(8,128)S(1)} %get-tuple-element.7.acc_ref, bf16[256,2048]{1,0:T(8,128)(2,1)S(1)} %get-tuple-element.8.last_ref, bf16[2048,256]{1,0:T(8,128)(2,1)S(1)} %get-tuple-element.9.turned_ref, f32[1,2048]{1,0:T(1,128)S(1)} %get-tuple-element.10.sums_ref, ...), custom_call_target="tpu_custom_call" | custom-call | tf_op jit(solution)/shard_map/finish/pallas_call | solution.py:269

commit v4 on v3

--- a/solution.py
+++ b/solution.py
@@ -65,7 +65,7 @@
 
 
 def round_of(shift):
-    return max(hops(shift), 1) if hops(shift) <= 2 else ROUNDS
+    return max(hops(shift), 1) if hops(shift) <= 2 or hops(shift) == 4 and shift % 2 else ROUNDS
 
 
 ORDER = [0] + send_order(round_of)

time: 65.7 us -> 65.6 us (level)
  no operation moved by 1% of the time
where the time goes in v4:
time: 65.6 us; the launch traced here: 64.9 us
  Pallas kernels  64.2 us (98%)
    pallas_call x1, Pallas kernels, local(): pl.pallas_call(gather_kernel, out_shape=(pltpu.VMEM((F, F), jnp.float32),...  57.4 us
    pallas_call x1, Pallas kernels, local(): pl.pallas_call(finish_kernel, out_shape=(jax.ShapeDtypeStruct((1, F), jnp...  6.85 us

profile of v4, /device:TPU:0, one launch (start us, length us, event | category | flops | bytes accessed | tf_op | source)
XLA Modules:
  0.0 64.9 jit_solution(15418692121524272855)
XLA Ops:
  0.6 57.4 %gather.1 = (f32[2048,2048]{1,0:T(8,128)S(1)}, bf16[256,2048]{1,0:T(8,128)(2,1)S(1)}, bf16[2048,256]{1,0:T(8,128)(2,1)S(1)}, f32[1,2048]{1,0:T(1,128)S(1)}, f32[1,128]{1,0:T(1,128)S(1)}) custom-call(s32[1,128]{1,0:T(1,128)} %bitcast.7, s32[8,128]{1,0:T(8,128)} %bitcast.6, bf16[128,8,2048]{2,1,0:T(8,128)(2,1)} %bitcast.5), custom_call_target="tpu_custom_call" | custom-call | tf_op jit(solution)/shard_map/gather/pallas_call | solution.py:233
  58.0 6.9 %finish.1 = (f32[1,2048]{1,0:T(1,128)}, f32[1,2048,2048]{2,1,0:T(8,128)}) custom-call(f32[2048,2048]{1,0:T(8,128)S(1)} %get-tuple-element.7.acc_ref, bf16[256,2048]{1,0:T(8,128)(2,1)S(1)} %get-tuple-element.8.last_ref, bf16[2048,256]{1,0:T(8,128)(2,1)S(1)} %get-tuple-element.9.turned_ref, f32[1,2048]{1,0:T(1,128)S(1)} %get-tuple-element.10.sums_ref, ...), custom_call_target="tpu_custom_call" | custom-call | tf_op jit(solution)/shard_map/finish/pallas_call | solution.py:269

commit v5 on v4

--- a/solution.py
+++ b/solution.py
@@ -51,7 +51,7 @@
     def score(shift):
         after = [a + b for a, b in zip(total, link_load(shift))]
         mean = sum(after) / 6
-        return round_of(shift) + (0, 0, 0, 1, 0.5, 0, 0)[hops(shift)], sum((a - mean) ** 2 for a in after), (shift * 37) % N
+        return round_of(shift) + (0, 0, 0, 1, 0.5, 0.2, 0)[hops(shift)], sum((a - mean) ** 2 for a in after), (shift * 37) % N
 
     while rest:
         best = min(rest, key=score)

time: 65.6 us -> 65.6 us (level)
  no operation moved by 1% of the time
where the time goes in v5:
time: 65.6 us; the launch traced here: 64.9 us
  Pallas kernels  64.2 us (98%)
    pallas_call x1, Pallas kernels, local(): pl.pallas_call(gather_kernel, out_shape=(pltpu.VMEM((F, F), jnp.float32),...  57.4 us
    pallas_call x1, Pallas kernels, local(): pl.pallas_call(finish_kernel, out_shape=(jax.ShapeDtypeStruct((1, F), jnp...  6.85 us

profile of v5, /device:TPU:0, one launch (start us, length us, event | category | flops | bytes accessed | tf_op | source)
XLA Modules:
  0.0 64.9 jit_solution(15418692121524272855)
XLA Ops:
  0.6 57.4 %gather.1 = (f32[2048,2048]{1,0:T(8,128)S(1)}, bf16[256,2048]{1,0:T(8,128)(2,1)S(1)}, bf16[2048,256]{1,0:T(8,128)(2,1)S(1)}, f32[1,2048]{1,0:T(1,128)S(1)}, f32[1,128]{1,0:T(1,128)S(1)}) custom-call(s32[1,128]{1,0:T(1,128)} %bitcast.7, s32[8,128]{1,0:T(8,128)} %bitcast.6, bf16[128,8,2048]{2,1,0:T(8,128)(2,1)} %bitcast.5), custom_call_target="tpu_custom_call" | custom-call | tf_op jit(solution)/shard_map/gather/pallas_call | solution.py:233
  58.0 6.9 %finish.1 = (f32[1,2048]{1,0:T(1,128)}, f32[1,2048,2048]{2,1,0:T(8,128)}) custom-call(f32[2048,2048]{1,0:T(8,128)S(1)} %get-tuple-element.7.acc_ref, bf16[256,2048]{1,0:T(8,128)(2,1)S(1)} %get-tuple-element.8.last_ref, bf16[2048,256]{1,0:T(8,128)(2,1)S(1)} %get-tuple-element.9.turned_ref, f32[1,2048]{1,0:T(1,128)S(1)} %get-tuple-element.10.sums_ref, ...), custom_call_target="tpu_custom_call" | custom-call | tf_op jit(solution)/shard_map/finish/pallas_call | solution.py:269
